TPU v7x, 256 devices: a whole 4x4x8 slice. The times are simulated.
256 devices in a mesh: xg: 4 (over x_hi, core), yd: 64 (over x_lo, z, y).
Axes of the slice: x: 4 (x_hi: 2, x_lo: 2; x = x_hi * 2 + x_lo), y: 4, z: 8, core: 2. Of those that a mesh axis runs over, the one named last changes fastest.
Arguments:
- mobile: float32 [4096, 1, 1024], P('yd', None, 'xg'), may hold values from 0 to 2
- dispersion_x: float32 [4096, 1, 1024], P('yd', None, 'xg'), may hold values from 0.5 to 200000
- dispersion_y: float32 [4096, 1, 1024], P('yd', None, 'xg'), may hold values from 0.5 to 200000
- capacity: float32 [4096, 1, 1024], P('yd', None, 'xg'), may hold values from 0.5 to 8
- immobile: float32 [4, 4096, 1, 1024], P(None, 'yd', None, 'xg'), may hold values from 0 to 2
- exchange_rates: float32 [4], replicated, may hold values from 0.02 to 50
- rate_shares: float32 [4], replicated, may hold values from 0.1 to 1
Outputs:
- updated: float32 [4096, 1, 1024], P('yd', None, 'xg')
All inputs are finite; a program needn't handle non-finite values.
Results may differ from a plain program's by a relative error of at most 0.0003.
Values sent between devices are 32-bit elements; how exact they have to be, the bound alone decides.
A program may use at most 64 MiB of HBM per device.

v0:
```python
import jax
import jax.numpy as jnp
from jax import lax
from jax.sharding import PartitionSpec as P


def shifted_2(value, axis, steps):
    count = lax.axis_size(axis)
    pairs = [(source, (source + steps) % count) for source in range(count)]
    return lax.ppermute(value, axis, pairs)


def shifted(values, stride, axis, filling):
    length = values.shape[axis]
    if stride > 0:
        kept_part = lax.slice_in_dim(values, 0, length - stride, axis=axis)
        filler = jnp.full_like(lax.slice_in_dim(values, 0, stride, axis=axis), filling)
        return jnp.concatenate([filler, kept_part], axis=axis)
    backward = -stride
    kept_part = lax.slice_in_dim(values, backward, length, axis=axis)
    filler = jnp.full_like(lax.slice_in_dim(values, 0, backward, axis=axis), filling)
    return jnp.concatenate([kept_part, filler], axis=axis)


def pick_at(values, position, axis):
    return lax.index_in_dim(values, position, axis, keepdims=False)


def periodic_solve(face_coef, storage, right_side, axis):
    length = right_side.shape[axis]
    sub_coef = -face_coef
    super_coef = -jnp.roll(face_coef, -1, axis)
    main_coef = storage + face_coef - super_coef
    stride = 1
    while stride < length // 2:
        sub_left = jnp.roll(sub_coef, stride, axis)
        main_left = jnp.roll(main_coef, stride, axis)
        super_left = jnp.roll(super_coef, stride, axis)
        side_left = jnp.roll(right_side, stride, axis)
        sub_right = jnp.roll(sub_coef, -stride, axis)
        main_right = jnp.roll(main_coef, -stride, axis)
        super_right = jnp.roll(super_coef, -stride, axis)
        side_right = jnp.roll(right_side, -stride, axis)
        left_ratio = sub_coef / main_left
        right_ratio = super_coef / main_right
        main_coef = main_coef - left_ratio * super_left - right_ratio * sub_right
        right_side = right_side - left_ratio * side_left - right_ratio * side_right
        sub_coef = -left_ratio * sub_left
        super_coef = -right_ratio * super_right
        stride = stride * 2
    coupling = sub_coef + super_coef
    main_other = jnp.roll(main_coef, stride, axis)
    coupling_other = jnp.roll(coupling, stride, axis)
    side_other = jnp.roll(right_side, stride, axis)
    return (right_side * main_other - coupling * side_other) / (
        main_coef * main_other - coupling * coupling_other
    )


def block_solve(face_coef, storage, source, axis):
    length = source.shape[axis]
    position = lax.broadcasted_iota(jnp.int32, source.shape, axis)
    at_first = position == 0
    at_last = position == length - 1
    following = shifted(face_coef, -1, axis, 0.0)
    nothing = jnp.zeros_like(source)
    sub_coef = jnp.where(at_first | at_last, nothing, -face_coef)
    super_coef = jnp.where(at_last, nothing, -following)
    main_coef = jnp.where(at_last, 1.0, storage + face_coef + following)
    right_side = jnp.stack(
        [
            jnp.where(at_last, nothing, source),
            jnp.where(at_first, face_coef, nothing),
            jnp.where(at_last, 1.0, nothing),
        ]
    )
    stride = 1
    while stride < length:
        sub_left = shifted(sub_coef, stride, axis, 0.0)
        main_left = shifted(main_coef, stride, axis, 1.0)
        super_left = shifted(super_coef, stride, axis, 0.0)
        side_left = shifted(right_side, stride, axis + 1, 0.0)
        sub_right = shifted(sub_coef, -stride, axis, 0.0)
        main_right = shifted(main_coef, -stride, axis, 1.0)
        super_right = shifted(super_coef, -stride, axis, 0.0)
        side_right = shifted(right_side, -stride, axis + 1, 0.0)
        left_ratio = sub_coef / main_left
        right_ratio = super_coef / main_right
        right_side = right_side - left_ratio[None] * side_left - right_ratio[None] * side_right
        main_coef = main_coef - left_ratio * super_left - right_ratio * sub_right
        sub_coef = -left_ratio * sub_left
        super_coef = -right_ratio * super_right
        stride = stride * 2
    return right_side / main_coef[None]


def reduced_rows(solved, face_coef, storage, source, upcoming, axis):
    from_next, face_next = upcoming
    length = source.shape[axis]
    face_last = pick_at(face_coef, length - 1, axis)
    sub_last = -face_last
    super_last = -face_next
    main_last = pick_at(storage, length - 1, axis) + face_last + face_next
    coef_prev = sub_last * pick_at(solved[1], length - 2, axis)
    coef_self = (
        main_last + sub_last * pick_at(solved[2], length - 2, axis) + super_last * from_next[1]
    )
    coef_next = super_last * from_next[2]
    target = (
        pick_at(source, length - 1, axis)
        - sub_last * pick_at(solved[0], length - 2, axis)
        - super_last * from_next[0]
    )
    return (coef_prev, coef_self, coef_next, target)


def dense_cyclic(all_rows, group_size):
    matrix_rows = []
    targets = []
    for row_index in range(group_size):
        entries = [jnp.zeros_like(all_rows[row_index, 1]) for column in range(group_size)]
        entries[(row_index - 1) % group_size] = all_rows[row_index, 0]
        entries[row_index] = all_rows[row_index, 1]
        entries[(row_index + 1) % group_size] = all_rows[row_index, 2]
        matrix_rows.append(entries)
        targets.append(all_rows[row_index, 3])
    for pivot in range(group_size):
        for row_index in range(pivot + 1, group_size):
            factor = matrix_rows[row_index][pivot] / matrix_rows[pivot][pivot]
            matrix_rows[row_index] = [
                matrix_rows[row_index][column] - factor * matrix_rows[pivot][column]
                for column in range(group_size)
            ]
            targets[row_index] = targets[row_index] - factor * targets[pivot]
    solutions = [None] * group_size
    for row_index in reversed(range(group_size)):
        total = targets[row_index]
        for column in range(row_index + 1, group_size):
            total = total - matrix_rows[row_index][column] * solutions[column]
        solutions[row_index] = total / matrix_rows[row_index][row_index]
    return jnp.stack(solutions)


def local(mobile, dispersion_x, dispersion_y, capacity, immobile, exchange_rates, rate_shares):
    weights = rate_shares * exchange_rates / (1.0 + exchange_rates)
    gain_terms = capacity[None] * weights[:, None, None, None]
    storage = 1.0 + jnp.sum(gain_terms, axis=0)
    source = mobile + jnp.sum(gain_terms * immobile, axis=0)
    solved = block_solve(dispersion_x, storage, source, 2)
    head_values = pick_at(solved, 0, 3)
    upcoming = shifted_2((head_values, pick_at(dispersion_x, 0, 2)), "xg", -1)
    rows = reduced_rows(solved, dispersion_x, storage, source, upcoming, 2)
    group_size = lax.axis_size("xg")
    all_rows = lax.all_gather(jnp.stack(rows)[None], "xg", axis=0, tiled=True)
    solutions = dense_cyclic(all_rows, group_size)
    own_index = lax.axis_index("xg")
    own_value = lax.dynamic_index_in_dim(solutions, own_index, 0, keepdims=False)
    prev_value = lax.dynamic_index_in_dim(
        solutions, (own_index + group_size - 1) % group_size, 0, keepdims=False
    )
    after_x = solved[0] + solved[1] * prev_value[..., None] + solved[2] * own_value[..., None]
    group_count = lax.axis_size("yd")

    def regroup(values):
        return values.reshape(values.shape[0], group_count, -1)

    line_values = lax.all_to_all(regroup(after_x), "yd", split_axis=1, concat_axis=0, tiled=True)
    line_faces = lax.all_to_all(
        regroup(dispersion_y), "yd", split_axis=1, concat_axis=0, tiled=True
    )
    line_storage = lax.all_to_all(regroup(storage), "yd", split_axis=1, concat_axis=0, tiled=True)
    solved_lines = periodic_solve(line_faces, line_storage, line_storage * line_values, 0)
    updated = lax.all_to_all(solved_lines, "yd", split_axis=0, concat_axis=1, tiled=True)
    updated = updated.reshape(after_x.shape)
    return updated


def solution(mesh):
    return jax.shard_map(
        local,
        mesh=mesh,
        in_specs=(
            P("yd", None, "xg"),
            P("yd", None, "xg"),
            P("yd", None, "xg"),
            P("yd", None, "xg"),
            P(None, "yd", None, "xg"),
            P(),
            P(),
        ),
        out_specs=P("yd", None, "xg"),
        check_vma=False,
    )
```

profile of v0, /device:TPU:4, one launch (start us, length us, event | category | flops | bytes accessed | tf_op | source)
XLA Modules:
  0.0 107.0 jit_solution(12925277914980473333)
XLA Ops:
  0.0 0.8 copy.95
  0.9 0.8 copy.55
  1.8 0.7 add_divide_fusion
  2.5 1.6 %fusion = (f32[64,256]{1,0:T(8,128)S(1)}, f32[64,256]{1,0:T(8,128)S(1)}) fusion(f32[4,64,1,256]{3,2,1,0:T(1,128)} %param.11, f32[64,256]{1,0:T(8,128)S(1)} %bitcast.400, f32[4]{0:T(128)S(1)} %add_divide_fusion), kind=kLoop, calls=%fused_computation.2 | loop fusion | flops 229376 | bytes 458768 | tf_op jit(solution)/shard_map/reduce_sum | solution.py:148
  4.1 0.9 add_select_fusion
  5.1 0.9 fusion.90
  11.8 0.6 slice_reduce_fusion.1
  12.3 2.4 %collective-permute-start = (f32[64,1]{0,1:T(1,128)S(1)}, f32[64,1]{0,1:T(1,128)S(1)}, u32[]{:S(2)}, u32[]{:S(2)}) collective-permute-start(f32[64,1]{0,1:T(1,128)S(1)} %bitcast.403), channel_id=1, source_target_pairs={{0,192},{64,0},{128,64},{192,128},{1,193},{65,1},{129,65},{193,129... | collective-permute-start | bytes 776 | tf_op jit(solution)/shard_map/ppermute | solution.py:10
  14.8 0.8 reshape.21111
  15.6 11.9 %all-to-all-start.2 = ((f32[64,1,256]{2,1,0:T(1,128)}), f32[64,1,256]{2,1,0:T(1,128)S(1)}, u32[]{:S(2)}, u32[]{:S(2)}) async-start(f32[64,1,256]{2,1,0:T(1,128)} %reshape.21111), calls=%async_computation.2 | async-start | bytes 131072 | tf_op jit(solution)/shard_map/all_to_all | solution.py:168
  27.6 0.2 fusion.53
  28.2 0.8 reshape.21113
  29.0 6.7 %all-gather = f32[16,64,1]{1,2,0:T(1,128)S(1)} all-gather(f32[4,64,1]{1,2,0:T(1,128)S(1)} %pad_maximum_fusion.2), channel_id=2, replica_groups=mesh['xg'=4,'yd'=64] {'xg'}, dimensions={0}, use_global_device_ids=true | all-gather | bytes 5120 | tf_op jit(solution)/shard_map/all_gather | solution.py:154
  35.9 0.8 reshape.21115
  36.6 1.7 %all-to-all-done.2 = f32[64,1,256]{2,1,0:T(1,128)S(1)} async-done(((f32[64,1,256]{2,1,0:T(1,128)}), f32[64,1,256]{2,1,0:T(1,128)S(1)}, u32[]{:S(2)}, u32[]{:S(2)}) %all-to-all-start.2) | async-done | bytes 65568 | tf_op jit(solution)/shard_map/all_to_all | solution.py:168
  38.3 9.6 %all-to-all-start = ((f32[64,1,256]{2,1,0:T(1,128)}), f32[64,1,256]{2,1,0:T(1,128)S(1)}, u32[]{:S(2)}, u32[]{:S(2)}) async-start(f32[64,1,256]{2,1,0:T(1,128)} %reshape.21113), calls=%async_computation | async-start | bytes 131072 | tf_op jit(solution)/shard_map/all_to_all | solution.py:171
  47.9 0.6 broadcast.430
  48.5 0.8 reduce.15
  49.6 9.1 %all-to-all-done = f32[64,1,256]{2,1,0:T(1,128)S(1)} async-done(((f32[64,1,256]{2,1,0:T(1,128)}), f32[64,1,256]{2,1,0:T(1,128)S(1)}, u32[]{:S(2)}, u32[]{:S(2)}) %all-to-all-start) | async-done | bytes 65568 | tf_op jit(solution)/shard_map/all_to_all | solution.py:171
  58.7 4.8 %all-to-all-start.1 = ((f32[64,1,256]{2,1,0:T(1,128)}), f32[64,1,256]{2,1,0:T(1,128)S(1)}, u32[]{:S(2)}, u32[]{:S(2)}) async-start(f32[64,1,256]{2,1,0:T(1,128)} %reshape.21115), calls=%async_computation.1 | async-start | bytes 131072 | tf_op jit(solution)/shard_map/all_to_all | solution.py:167
  63.5 0.8 reduce.14
  64.5 9.5 %all-to-all-done.1 = f32[64,1,256]{2,1,0:T(1,128)S(1)} async-done(((f32[64,1,256]{2,1,0:T(1,128)}), f32[64,1,256]{2,1,0:T(1,128)S(1)}, u32[]{:S(2)}, u32[]{:S(2)}) %all-to-all-start.1) | async-done | bytes 65568 | tf_op jit(solution)/shard_map/all_to_all | solution.py:167
  74.1 0.8 reduce.16
  81.5 0.2 fusion.26
  83.7 0.6 reduce.17
  84.3 0.6 copy.96
  85.0 1.7 %reshape.21117 = f32[64,1,256]{2,1,0:T(1,128)S(1)} reshape(f32[4096,4]{1,0:T(8,128)S(1)} %copy.96) | data formatting | bytes 131072
  86.7 14.6 %all_to_all.69 = f32[64,1,256]{2,1,0:T(1,128)S(1)} all-to-all(f32[64,1,256]{2,1,0:T(1,128)S(1)} %reshape.21117), channel_id=1, replica_groups=mesh['xg'=4,'yd'=64] {'yd'}, dimensions={0} | all-to-all | bytes 131072 | tf_op jit(solution)/shard_map/all_to_all | solution.py:173
  101.3 0.8 reduce.18
  102.1 3.4 %reshape.21118 = f32[4096,1,4]{2,1,0:T(1,128)S(1)} reshape(f32[64,256]{1,0:T(8,128)S(1)} %reduce.18) | data formatting | bytes 131072
  105.5 0.7 copy.86
  106.3 0.7 copy.85
  (220 shorter events, 15.0 us)
Async XLA Ops:
  0.0 6.0 %copy-start = (f32[64,1,256]{2,1,0:T(1,128)S(1)}, f32[64,1,256]{2,1,0:T(1,128)}, u32[]{:S(2)}) copy-start(f32[64,1,256]{2,1,0:T(1,128)} %param.8) | copy-start | bytes 196612
  11.1 3.6 %copy-start.1 = (f32[64,1,256]{2,1,0:T(1,128)S(1)}, f32[64,1,256]{2,1,0:T(1,128)}, u32[]{:S(2)}) copy-start(f32[64,1,256]{2,1,0:T(1,128)} %param.9) | copy-start | bytes 196612
  11.7 17.3 %collective-permute-start.1 = (f32[3,64,1]{1,2,0:T(1,128)S(1)}, f32[3,64,1]{1,2,0:T(1,128)S(1)}, u32[]{:S(2)}, u32[]{:S(2)}) collective-permute-start(f32[3,64,1]{1,2,0:T(1,128)S(1)} %squeeze.95), channel_id=1, source_target_pairs={{0,192},{64,0},{128,64},{192,128},{1,193},{65,1},{129,65},{193,129... | collective-permute-start | bytes 2312 | tf_op jit(solution)/shard_map/ppermute | solution.py:10
  12.3 16.7 %collective-permute-start = (f32[64,1]{0,1:T(1,128)S(1)}, f32[64,1]{0,1:T(1,128)S(1)}, u32[]{:S(2)}, u32[]{:S(2)}) collective-permute-start(f32[64,1]{0,1:T(1,128)S(1)} %bitcast.403), channel_id=1, source_target_pairs={{0,192},{64,0},{128,64},{192,128},{1,193},{65,1},{129,65},{193,129... | collective-permute-start | bytes 776 | tf_op jit(solution)/shard_map/ppermute | solution.py:10
  15.6 22.7 %all-to-all-start.2 = ((f32[64,1,256]{2,1,0:T(1,128)}), f32[64,1,256]{2,1,0:T(1,128)S(1)}, u32[]{:S(2)}, u32[]{:S(2)}) async-start(f32[64,1,256]{2,1,0:T(1,128)} %reshape.21111), calls=%async_computation.2 | async-start | bytes 131072 | tf_op jit(solution)/shard_map/all_to_all | solution.py:168
  38.3 20.4 %all-to-all-start = ((f32[64,1,256]{2,1,0:T(1,128)}), f32[64,1,256]{2,1,0:T(1,128)S(1)}, u32[]{:S(2)}, u32[]{:S(2)}) async-start(f32[64,1,256]{2,1,0:T(1,128)} %reshape.21113), calls=%async_computation | async-start | bytes 131072 | tf_op jit(solution)/shard_map/all_to_all | solution.py:171
  58.7 15.4 %all-to-all-start.1 = ((f32[64,1,256]{2,1,0:T(1,128)}), f32[64,1,256]{2,1,0:T(1,128)S(1)}, u32[]{:S(2)}, u32[]{:S(2)}) async-start(f32[64,1,256]{2,1,0:T(1,128)} %reshape.21115), calls=%async_computation.1 | async-start | bytes 131072 | tf_op jit(solution)/shard_map/all_to_all | solution.py:167
where the time goes:
time: 108 us; the launch traced here: 107 us
  starting transfers between devices  28.8 us (27%)
  local copies, waits for them, and re-layouts  21.3 us (20%)
  blocking collectives  21.3 us (20%)
  waiting for transfers between devices  20.3 us (19%)
  other arithmetic  14.1 us (13%)
  between operations  1.29 us (1%)
    all_to_all x1, blocking collectives, local(): lax.all_to_all(solved_lines, 'yd', split_axis=0, concat_axis=1, tiled=True)  14.6 us
    all_to_all x1, starting transfers between devices, local(): lax.all_to_all(regroup(dispersion_y), 'yd', split_axis=1, concat_axis=0,...  11.9 us
    unnamed x16, local copies, waits for them, and re-layouts  10.2 us
    all_to_all x1, starting transfers between devices, local(): lax.all_to_all(regroup(storage), 'yd', split_axis=1, concat_axis=0, tiled...  9.63 us
    all_to_all x1, waiting for transfers between devices, local(): lax.all_to_all(regroup(after_x), 'yd', split_axis=1, concat_axis=0, tiled...  9.53 us
    all_to_all x1, waiting for transfers between devices, local(): lax.all_to_all(regroup(storage), 'yd', split_axis=1, concat_axis=0, tiled...  9.06 us
    all_gather x1, blocking collectives, local(): all_rows = lax.all_gather(jnp.stack(rows)[None], 'xg', axis=0, tiled=True)  6.7 us
    all_to_all x1, starting transfers between devices, local(): lax.all_to_all(regroup(after_x), 'yd', split_axis=1, concat_axis=0, tiled...  4.8 us
  transfers between devices with their start and end apart: 5, of which 3 were waited for; matrix products, arithmetic and copies ran while one was open for 6% of the time, Pallas kernels for 0%

commit v1 on v0

--- a/solution.py
+++ b/solution.py
@@ -170,7 +170,10 @@
     )
     line_storage = lax.all_to_all(regroup(storage), "yd", split_axis=1, concat_axis=0, tiled=True)
     solved_lines = periodic_solve(line_faces, line_storage, line_storage * line_values, 0)
-    updated = lax.all_to_all(solved_lines, "yd", split_axis=0, concat_axis=1, tiled=True)
+    updated = jnp.concatenate(
+        lax.all_to_all(jnp.stack(jnp.split(solved_lines, lax.axis_size("yd"), axis=0)), "yd", 0, 0),
+        axis=1,
+    )
     updated = updated.reshape(after_x.shape)
     return updated
 

time: 108 us -> 102 us (0.944)
  other arithmetic: 14.1 us -> 10.3 us
  local copies, waits for them, and re-layouts: 21.3 us -> 19.1 us
  waiting for transfers between devices: 20.3 us -> 18.5 us
  blocking collectives: 21.3 us -> 22.5 us
  starting transfers between devices: 28.8 us -> 30 us
    all_to_all x1, starting transfers between devices: 9.63 us -> 11.3 us  [local(): lax.all_to_all(regroup(storage), 'yd', split_axis=1, concat_axis=0, tiled...]
    all_to_all x1, waiting for transfers between devices: 1.66 us -> 0.01 us  [local(): lax.all_to_all(regroup(dispersion_y), 'yd', split_axis=1, concat_axis=0,...]
    unnamed x16 -> x86, local copies, waits for them, and re-layouts: 10.2 us -> 8.61 us
    ppermute x2, starting transfers between devices: 2.44 us -> 1.04 us  [shifted_2(): return lax.ppermute(value, axis, pairs)]
    all_gather x1, blocking collectives: 6.7 us -> 7.96 us  [local(): all_rows = lax.all_gather(jnp.stack(rows)[None], 'xg', axis=0, tiled=True)]
  transfers between devices with their start and end apart: 5 -> 5, of which waited for: 3 -> 2; matrix products, arithmetic and copies ran while one was open for 6% -> 12% of each run, Pallas kernels for 0% -> 0%
where the time goes in v1:
time: 102 us
  starting transfers between devices  30 us (29%)
  blocking collectives  22.5 us (22%)
  local copies, waits for them, and re-layouts  19.1 us (19%)
  waiting for transfers between devices  18.5 us (18%)
  other arithmetic  10.3 us (10%)
  between operations  1.36 us (1%)
    all_to_all x1, blocking collectives, local(): lax.all_to_all(jnp.stack(jnp.split(solved_lines, lax.axis_size('yd'), axi...  14.6 us
    all_to_all x1, starting transfers between devices, local(): lax.all_to_all(regroup(dispersion_y), 'yd', split_axis=1, concat_axis=0,...  12.9 us
    all_to_all x1, starting transfers between devices, local(): lax.all_to_all(regroup(storage), 'yd', split_axis=1, concat_axis=0, tiled...  11.3 us
    all_to_all x1, waiting for transfers between devices, local(): lax.all_to_all(regroup(after_x), 'yd', split_axis=1, concat_axis=0, tiled...  9.5 us
    all_to_all x1, waiting for transfers between devices, local(): lax.all_to_all(regroup(storage), 'yd', split_axis=1, concat_axis=0, tiled...  8.99 us
    unnamed x86, local copies, waits for them, and re-layouts  8.61 us
    all_gather x1, blocking collectives, local(): all_rows = lax.all_gather(jnp.stack(rows)[None], 'xg', axis=0, tiled=True)  7.96 us
    all_to_all x1, starting transfers between devices, local(): lax.all_to_all(regroup(after_x), 'yd', split_axis=1, concat_axis=0, tiled...  4.78 us
  transfers between devices with their start and end apart: 5, of which 2 were waited for; matrix products, arithmetic and copies ran while one was open for 12% of the time, Pallas kernels for 0%

profile of v1, /device:TPU:4, one launch (start us, length us, event | category | flops | bytes accessed | tf_op | source)
XLA Modules:
  0.0 101.7 jit_solution(14564751586257472106)
XLA Ops:
  0.0 0.9 copy.232
  0.9 0.8 reshape.21110
  1.7 12.9 %all-to-all-start.2 = ((f32[64,1,256]{2,1,0:T(1,128)}), f32[64,1,256]{2,1,0:T(1,128)S(1)}, u32[]{:S(2)}, u32[]{:S(2)}) async-start(f32[64,1,256]{2,1,0:T(1,128)} %reshape.21110), calls=%async_computation.2 | async-start | bytes 131072 | tf_op jit(solution)/shard_map/all_to_all | solution.py:168
  14.7 0.8 copy-done
  15.6 0.6 copy-done.4
  16.2 0.7 fusion
  17.1 0.7 copy-done.2
  23.6 0.6 slice_reduce_fusion.1
  24.1 1.0 collective-permute-start
  25.1 0.2 fusion.53
  25.5 0.8 reshape.21112
  26.6 8.0 %all-gather = f32[16,64,1]{1,2,0:T(1,128)S(1)} all-gather(f32[4,64,1]{1,2,0:T(1,128)S(1)} %pad_maximum_fusion.2), channel_id=2, replica_groups=mesh['xg'=4,'yd'=64] {'xg'}, dimensions={0}, use_global_device_ids=true | all-gather | bytes 5120 | tf_op jit(solution)/shard_map/all_gather | solution.py:154
  34.7 0.8 reshape.21114
  35.5 11.3 %all-to-all-start = ((f32[64,1,256]{2,1,0:T(1,128)}), f32[64,1,256]{2,1,0:T(1,128)S(1)}, u32[]{:S(2)}, u32[]{:S(2)}) async-start(f32[64,1,256]{2,1,0:T(1,128)} %reshape.21112), calls=%async_computation | async-start | bytes 131072 | tf_op jit(solution)/shard_map/all_to_all | solution.py:171
  46.8 0.6 broadcast.430
  47.3 0.8 reduce.15
  48.5 9.0 %all-to-all-done = f32[64,1,256]{2,1,0:T(1,128)S(1)} async-done(((f32[64,1,256]{2,1,0:T(1,128)}), f32[64,1,256]{2,1,0:T(1,128)S(1)}, u32[]{:S(2)}, u32[]{:S(2)}) %all-to-all-start) | async-done | bytes 65568 | tf_op jit(solution)/shard_map/all_to_all | solution.py:171
  57.5 4.8 %all-to-all-start.1 = ((f32[64,1,256]{2,1,0:T(1,128)}), f32[64,1,256]{2,1,0:T(1,128)S(1)}, u32[]{:S(2)}, u32[]{:S(2)}) async-start(f32[64,1,256]{2,1,0:T(1,128)} %reshape.21114), calls=%async_computation.1 | async-start | bytes 131072 | tf_op jit(solution)/shard_map/all_to_all | solution.py:167
  62.3 0.8 reduce.14
  63.4 9.5 %all-to-all-done.1 = f32[64,1,256]{2,1,0:T(1,128)S(1)} async-done(((f32[64,1,256]{2,1,0:T(1,128)}), f32[64,1,256]{2,1,0:T(1,128)S(1)}, u32[]{:S(2)}, u32[]{:S(2)}) %all-to-all-start.1) | async-done | bytes 65568 | tf_op jit(solution)/shard_map/all_to_all | solution.py:167
  72.9 0.8 reduce.16
  74.6 0.1 fusion.2
  75.4 0.2 fusion.6
  76.4 0.2 fusion.10
  77.4 0.2 fusion.14
  78.4 0.2 fusion.18
  79.4 0.2 fusion.22
  80.4 0.2 fusion.26
  81.8 0.1 fusion.38
  85.5 14.6 %all_to_all.59 = f32[64,1,256]{2,1,0:T(1,128)S(1)} all-to-all(f32[64,1,256]{2,1,0:T(1,128)S(1)} %reshape.21116), channel_id=1, replica_groups=mesh['xg'=4,'yd'=64] {'yd'}, dimensions={0} | all-to-all | bytes 131072 | tf_op jit(solution)/shard_map/all_to_all | solution.py:174
  100.1 0.8 reduce.17
  101.0 0.7 copy.234
  (288 shorter events, 16.6 us)
Async XLA Ops:
  0.9 15.2 %copy-start.1 = (f32[4,64,1,256]{3,2,1,0:T(1,128)S(1)}, f32[4,64,1,256]{3,2,1,0:T(1,128)}, u32[]{:S(2)}) copy-start(f32[4,64,1,256]{3,2,1,0:T(1,128)} %param.11) | copy-start | bytes 786436
  1.7 12.9 %copy-start.3 = (f32[64,1,256]{2,1,0:T(1,128)S(1)}, f32[64,1,256]{2,1,0:T(1,128)}, u32[]{:S(2)}) copy-start(f32[64,1,256]{2,1,0:T(1,128)} %param.10) | copy-start | bytes 196612
  1.7 33.7 %all-to-all-start.2 = ((f32[64,1,256]{2,1,0:T(1,128)}), f32[64,1,256]{2,1,0:T(1,128)S(1)}, u32[]{:S(2)}, u32[]{:S(2)}) async-start(f32[64,1,256]{2,1,0:T(1,128)} %reshape.21110), calls=%async_computation.2 | async-start | bytes 131072 | tf_op jit(solution)/shard_map/all_to_all | solution.py:168
  14.7 0.8 copy-start
  15.5 0.7 copy-start.4
  15.5 0.7 copy-start.5
  17.0 0.8 copy-start.2
  23.5 3.1 %collective-permute-start.1 = (f32[3,64,1]{1,2,0:T(1,128)S(1)}, f32[3,64,1]{1,2,0:T(1,128)S(1)}, u32[]{:S(2)}, u32[]{:S(2)}) collective-permute-start(f32[3,64,1]{1,2,0:T(1,128)S(1)} %squeeze.95), channel_id=1, source_target_pairs={{0,192},{64,0},{128,64},{192,128},{1,193},{65,1},{129,65},{193,129... | collective-permute-start | bytes 2312 | tf_op jit(solution)/shard_map/ppermute | solution.py:10
  24.1 2.4 %collective-permute-start = (f32[64,1]{0,1:T(1,128)S(1)}, f32[64,1]{0,1:T(1,128)S(1)}, u32[]{:S(2)}, u32[]{:S(2)}) collective-permute-start(f32[64,1]{0,1:T(1,128)S(1)} %bitcast.660), channel_id=1, source_target_pairs={{0,192},{64,0},{128,64},{192,128},{1,193},{65,1},{129,65},{193,129... | collective-permute-start | bytes 776 | tf_op jit(solution)/shard_map/ppermute | solution.py:10
  35.5 22.1 %all-to-all-start = ((f32[64,1,256]{2,1,0:T(1,128)}), f32[64,1,256]{2,1,0:T(1,128)S(1)}, u32[]{:S(2)}, u32[]{:S(2)}) async-start(f32[64,1,256]{2,1,0:T(1,128)} %reshape.21112), calls=%async_computation | async-start | bytes 131072 | tf_op jit(solution)/shard_map/all_to_all | solution.py:171
  57.5 15.4 %all-to-all-start.1 = ((f32[64,1,256]{2,1,0:T(1,128)}), f32[64,1,256]{2,1,0:T(1,128)S(1)}, u32[]{:S(2)}, u32[]{:S(2)}) async-start(f32[64,1,256]{2,1,0:T(1,128)} %reshape.21114), calls=%async_computation.1 | async-start | bytes 131072 | tf_op jit(solution)/shard_map/all_to_all | solution.py:167
